TPU v7x, 32 devices: a whole 2x2x4 slice. The times are simulated.
32 devices in a mesh: ctx: 16 (over z, y, x), tp: 2 (over core).
Axes of the slice: x: 2, y: 2, z: 4, core: 2. Of those that a mesh axis runs over, the one named last changes fastest.
Arguments:
- tokens: bfloat16 [4096, 2688], P(('ctx', 'tp')), may hold values from -6 to 6
- result_grad: bfloat16 [4096, 2688], P(('ctx', 'tp')), may hold values from -6 to 6
- query_weight: bfloat16 [2688, 512], P(None, 'tp'), may hold values from -0.125 to 0.125
- key_weight: bfloat16 [2688, 256], P(None, 'tp'), may hold values from -0.125 to 0.125
- value_weight: bfloat16 [2688, 256], P(None, 'tp'), may hold values from -0.125 to 0.125
- output_weight: bfloat16 [512, 2688], P('tp'), may hold values from -0.5 to 0.5
- query_gain: float32 [128], replicated, may hold values from 0.5 to 1.5
- key_gain: float32 [128], replicated, may hold values from 0.5 to 1.5
Outputs:
- layer_output: bfloat16 [4096, 2688], P(('ctx', 'tp'))
- tokens_grad: bfloat16 [4096, 2688], P(('ctx', 'tp'))
All inputs are finite; a program needn't handle non-finite values.
Results may differ from a plain program's by a relative error of at most 0.012.
Values may be sent and summed in bfloat16 or wider, within the bound.
A program may use at most 64 MiB of HBM per device.

v0:
```python
import jax
import jax.numpy as jnp
from jax import lax
from jax.sharding import PartitionSpec as P

WINDOW = 1024
norm_epsilon = 1e-06
score_scale = 168.0 ** (-0.5)
rope_theta = 10000.0


def from_behind(block, axis, distance):
    devices = range(lax.axis_size(axis))
    route = [(i - distance, i) for i in devices if i - distance in devices]
    return lax.ppermute(block, axis, route)


def rope_tables(positions, head_size):
    half_size = head_size // 2
    exponent = jnp.arange(half_size, dtype=jnp.float32) * (2.0 / head_size)
    frequency = jnp.power(jnp.float32(rope_theta), -exponent)
    angles = positions.astype(jnp.float32)[:, None] * frequency[None, :]
    return (jnp.cos(angles), jnp.sin(angles))


def norm_rope(raw_proj, scale_gain, cosines, sines):
    row_count = raw_proj.shape[0]
    head_size = scale_gain.shape[0]
    split_heads = raw_proj.reshape(row_count, -1, head_size)
    mean_square = jnp.mean(split_heads * split_heads, axis=-1, keepdims=True)
    normed = split_heads * lax.rsqrt(mean_square + norm_epsilon) * scale_gain
    half_size = head_size // 2
    low_half = normed[..., :half_size]
    high_half = normed[..., half_size:]
    cosine_b = cosines[:, None, :]
    sine_b = sines[:, None, :]
    return jnp.concatenate(
        [low_half * cosine_b - high_half * sine_b, high_half * cosine_b + low_half * sine_b],
        axis=-1,
    )


def attend(queries, keys_all, values_all, out_grad, query_first, key_first):
    query_count = queries.shape[0]
    key_count = keys_all.shape[0]
    scores = (
        jnp.einsum("qkgh,ckh->kgqc", queries, keys_all, preferred_element_type=jnp.float32)
        * score_scale
    )
    query_pos = query_first + jnp.arange(query_count, dtype=jnp.int32)
    key_pos = key_first + jnp.arange(key_count, dtype=jnp.int32)
    distance = query_pos[:, None] - key_pos[None, :]
    allowed = (distance >= 0) & (distance < WINDOW) & (key_pos[None, :] >= 0)
    weights_raw = jnp.where(allowed, jnp.exp(scores), jnp.float32(0.0))
    denominator = jnp.sum(weights_raw, axis=-1, keepdims=True)
    weights_soft = weights_raw / denominator
    weights_low = weights_soft.astype(jnp.bfloat16)
    attended_wide = jnp.einsum(
        "kgqc,ckh->qkgh", weights_low, values_all, preferred_element_type=jnp.float32
    )
    attended = lax.optimization_barrier(attended_wide.astype(jnp.bfloat16))
    row_dots = jnp.sum(out_grad.astype(jnp.float32) * attended.astype(jnp.float32), axis=-1)
    prob_grad = jnp.einsum(
        "qkgh,ckh->kgqc", out_grad, values_all, preferred_element_type=jnp.float32
    )
    centered = prob_grad - jnp.transpose(row_dots, (1, 2, 0))[..., None]
    score_grad = (weights_soft * centered * score_scale).astype(jnp.bfloat16)
    query_grad = jnp.einsum(
        "kgqc,ckh->qkgh", score_grad, keys_all, preferred_element_type=jnp.float32
    )
    key_grad = jnp.einsum("kgqc,qkgh->ckh", score_grad, queries, preferred_element_type=jnp.float32)
    value_grad = jnp.einsum(
        "kgqc,qkgh->ckh", weights_low, out_grad, preferred_element_type=jnp.float32
    )
    return (attended, query_grad, key_grad, value_grad)


def on_device(
    tokens, result_grad, query_weight, key_weight, value_weight, output_weight, query_gain, key_gain
):
    local_rows = tokens.shape[0]
    row_count = local_rows * lax.axis_size("tp")
    head_size = query_gain.shape[0]
    query_cols = query_weight.shape[1]
    kv_cols = key_weight.shape[1]
    kv_count = kv_cols // head_size
    per_kv = query_cols // kv_cols
    stacked = jnp.stack([tokens, result_grad])
    portion = lax.all_gather(stacked, "tp", axis=1, tiled=True)
    inputs_part = portion[0]
    gradients_part = portion[1]
    query_rows = jnp.dot(inputs_part, query_weight, preferred_element_type=jnp.float32)
    key_rows = jnp.dot(inputs_part, key_weight, preferred_element_type=jnp.float32)
    value_rows = jnp.dot(inputs_part, value_weight, preferred_element_type=jnp.float32)
    grad_rows = jnp.einsum(
        "nd,hd->nh", gradients_part, output_weight, preferred_element_type=jnp.float32
    )
    joined = jnp.concatenate([query_rows, key_rows, value_rows, grad_rows], axis=1)
    query_raw = joined[:, :query_cols]
    key_raw = joined[:, query_cols : query_cols + kv_cols]
    value_raw = joined[:, query_cols + kv_cols : query_cols + 2 * kv_cols]
    out_grad = (
        joined[:, query_cols + 2 * kv_cols :]
        .astype(jnp.bfloat16)
        .reshape(row_count, kv_count, per_kv, head_size)
    )
    row_first = lax.axis_index("ctx") * row_count
    positions = row_first + jnp.arange(row_count, dtype=jnp.int32)
    cosines, sines = rope_tables(positions, head_size)
    queries = (
        norm_rope(query_raw, query_gain, cosines, sines)
        .astype(jnp.bfloat16)
        .reshape(row_count, kv_count, per_kv, head_size)
    )
    keys_own = norm_rope(key_raw, key_gain, cosines, sines).astype(jnp.bfloat16)
    values_own = value_raw.astype(jnp.bfloat16).reshape(row_count, kv_count, head_size)
    tail_rows = min(row_count, WINDOW)
    reach = WINDOW // tail_rows
    own_tail = jnp.stack([keys_own, values_own])
    arrivals = []
    message = own_tail
    for stride in range(1, reach + 1):
        sender = own_tail
        distance = stride
        message = from_behind(sender, "ctx", distance)
        arrivals.append(message)
    halo_rows = jnp.concatenate(arrivals[::-1], axis=1)
    keys_all = jnp.concatenate([halo_rows[0], keys_own], axis=0)
    values_all = jnp.concatenate([halo_rows[1], values_own], axis=0)
    attended, query_grad, key_grad, value_grad = attend(
        queries, keys_all, values_all, out_grad, row_first, row_first - WINDOW
    )
    attended_flat = attended.reshape(row_count, query_cols)
    halo_grad = jnp.stack([key_grad[:WINDOW], value_grad[:WINDOW]])
    returned = jnp.zeros((2, tail_rows, kv_count, head_size), jnp.float32)
    for turn_index in range(reach):
        portion_stride = turn_index + 1
        sender = halo_grad[
            :, WINDOW - portion_stride * tail_rows : WINDOW - (portion_stride - 1) * tail_rows
        ]
        distance = -(turn_index + 1)
        arrived = from_behind(sender.astype(jnp.bfloat16), "ctx", distance).astype(sender.dtype)
        returned = returned + arrived
    keep_rows = row_count - tail_rows
    key_grad_own = key_grad[WINDOW:]
    value_grad_own = value_grad[WINDOW:]
    key_grad_own = jnp.concatenate([key_grad_own[:keep_rows], key_grad_own + returned[0]], axis=0)
    value_grad_own = jnp.concatenate(
        [value_grad_own[:keep_rows], value_grad_own + returned[1]], axis=0
    )

    def query_shape(raw_proj):
        return norm_rope(raw_proj, query_gain, cosines, sines)

    def key_shape(raw_proj):
        return norm_rope(raw_proj, key_gain, cosines, sines)

    query_back = jax.vjp(query_shape, query_raw)[1](query_grad.reshape(row_count, -1, head_size))[
        0
    ].astype(jnp.bfloat16)
    key_back = jax.vjp(key_shape, key_raw)[1](key_grad_own)[0].astype(jnp.bfloat16)
    value_back = value_grad_own.reshape(row_count, kv_cols).astype(jnp.bfloat16)
    out_part = jnp.dot(attended_flat, output_weight, preferred_element_type=jnp.float32)
    query_rows = query_back
    key_rows = key_back
    value_rows = value_back
    summed = jnp.einsum("nh,dh->nd", query_rows, query_weight, preferred_element_type=jnp.float32)
    summed = summed + jnp.einsum(
        "nh,dh->nd", key_rows, key_weight, preferred_element_type=jnp.float32
    )
    summed = summed + jnp.einsum(
        "nh,dh->nd", value_rows, value_weight, preferred_element_type=jnp.float32
    )
    out_sum, grad_sum = (
        lax.psum_scatter(
            out_part.astype(jnp.bfloat16), "tp", scatter_dimension=0, tiled=True
        ).astype(jnp.float32),
        lax.psum_scatter(summed.astype(jnp.bfloat16), "tp", scatter_dimension=0, tiled=True).astype(
            jnp.float32
        ),
    )
    layer_output = (tokens.astype(jnp.float32) + out_sum).astype(jnp.bfloat16)
    tokens_grad = (result_grad.astype(jnp.float32) + grad_sum).astype(jnp.bfloat16)
    return (layer_output, tokens_grad)


def solution(mesh):
    in_specs = (
        P(("ctx", "tp"), None),
        P(("ctx", "tp"), None),
        P(None, "tp"),
        P(None, "tp"),
        P(None, "tp"),
        P("tp", None),
        P(),
        P(),
    )
    out_specs = (P(("ctx", "tp"), None), P(("ctx", "tp"), None))
    return jax.shard_map(
        on_device, mesh=mesh, in_specs=in_specs, out_specs=out_specs, check_vma=False
    )
```

profile of v0, /device:TPU:0, one launch (start us, length us, event | category | flops | bytes accessed | tf_op | source)
XLA Modules:
  0.0 92.2 jit_solution(1839996132509159438)
XLA Ops:
  7.2 0.0 copy-start
  7.2 0.0 all-gather.2.cloned.1.call-start
  7.2 2.7 %pad_maximum_fusion = bf16[2,128,2688]{2,1,0:T(8,128)(2,1)} fusion(bf16[1,128,2688]{2,1,0:T(8,128)(2,1)} %bitcast.158, bf16[1,128,2688]{2,1,0:T(8,128)(2,1)} %bitcast.157), kind=kLoop, calls=%fused_computation.20 | loop fusion | flops 688128 | bytes 2752512 | tf_op jit(solution)/shard_map/stack | solution.py:88
  9.9 0.0 all-gather.2.cloned.1.call-update
  9.9 0.0 reduce-scatter.3.cloned.1.call-start
  10.0 1.3 %copy-done.1 = bf16[2688,256]{1,0:T(8,128)(2,1)S(1)} copy-done((bf16[2688,256]{1,0:T(8,128)(2,1)S(1)}, bf16[2688,256]{1,0:T(8,128)(2,1)}, u32[]{:S(2)}) %copy-start.1) | copy-done | bytes 1376280
  11.2 1.7 %copy.30 = bf16[256,2688]{1,0:T(8,128)(2,1)} copy(bf16[256,2688]{0,1:T(8,128)(2,1)S(1)} %bitcast.156) | data formatting | bytes 2752512 | tf_op jit(solution)/shard_map/dot_general | solution.py:92
  12.9 0.0 copy-start.11
  13.0 0.3 multiply_cosine_fusion
  13.3 1.6 %fusion.20 = pred[256,1280]{0,1:T(8,128)(4,1)} fusion(s32[1280]{0:T(1024)S(1)} %iota_add_fusion, s32[256]{0:T(256)S(1)} %iota_add_fusion.1, pred[1280]{0:T(1024)(128)(4,1)S(1)} %broadcast_compare_fusion), kind=kLoop, calls=%fused_computation.34 | loop fusion | flops 1638400 | bytes 335104 | tf_op jit(solution)/shard_map/and | solution.py:53
  14.9 9.5 %all-gather.2.cloned.1.call-done = bf16[2,256,2688]{2,1,0:T(8,128)(2,1)} async-done(((bf16[2,128,2688]{2,1,0:T(8,128)(2,1)}), bf16[2,256,2688]{2,1,0:T(8,128)(2,1)}) %all-gather.2.cloned.1.call-update) | async-done | bytes 2752528 | tf_op jit(solution)/shard_map/all_gather | solution.py:89
  24.3 2.3 %multiply_reduce_fusion.2 = (f32[256]{0:T(256)S(1)}, f32[256,128]{0,1:T(8,128)S(1)}) fusion(bf16[2688,128]{1,0:T(8,128)(2,1)} %param.11, bf16[2,256,2688]{2,1,0:T(8,128)(2,1)} %all-gather.2.cloned.1.call-done), kind=kOutput, calls=%fused_computation.77 | convolution fusion | flops 176226048 | bytes 2196480 | tf_op jit(solution)/shard_map/dot_general | solution.py:93
  26.6 0.1 multiply_bitcast_fusion
  26.8 0.3 fusion.51
  27.1 2.0 %fusion.28 = bf16[256,128]{0,1:T(8,128)(2,1)S(1)} fusion(bf16[2688,128]{1,0:T(8,128)(2,1)S(1)} %copy-done.8, bf16[2,256,2688]{2,1,0:T(8,128)(2,1)} %all-gather.2.cloned.1.call-done), kind=kOutput, calls=%fused_computation.39 | convolution fusion | flops 176193536 | bytes 2129920 | tf_op jit(solution)/shard_map/dot_general | solution.py:94
  29.1 3.6 %collective-permute-start.3 = (bf16[2,256,1,128]{1,3,2,0:T(8,128)(2,1)S(1)}, bf16[2,256,1,128]{1,3,2,0:T(8,128)(2,1)S(1)}, u32[]{:S(2)}, u32[]{:S(2)}) collective-permute-start(bf16[2,256,1,128]{1,3,2,0:T(8,128)(2,1)S(1)} %pad_maximum_fusion.1), channel_id=1, source_target_pairs={{0,2},{2,4},{4,6},{6,8},{8,10},{10,12},{12,14},{14,16},{16,18},{18... | collective-permute-start | bytes 393224 | tf_op jit(solution)/shard_map/ppermute | solution.py:15
  32.8 3.4 %collective-permute-start.2 = (bf16[2,256,1,128]{1,3,2,0:T(8,128)(2,1)S(1)}, bf16[2,256,1,128]{1,3,2,0:T(8,128)(2,1)S(1)}, u32[]{:S(2)}, u32[]{:S(2)}) collective-permute-start(bf16[2,256,1,128]{1,3,2,0:T(8,128)(2,1)S(1)} %pad_maximum_fusion.1), channel_id=1, source_target_pairs={{0,4},{2,6},{4,8},{6,10},{8,12},{10,14},{12,16},{14,18},{16,20},{1... | collective-permute-start | bytes 393224 | tf_op jit(solution)/shard_map/ppermute | solution.py:15
  36.2 4.3 %collective-permute-start.1 = (bf16[2,256,1,128]{1,3,2,0:T(8,128)(2,1)S(1)}, bf16[2,256,1,128]{1,3,2,0:T(8,128)(2,1)S(1)}, u32[]{:S(2)}, u32[]{:S(2)}) collective-permute-start(bf16[2,256,1,128]{1,3,2,0:T(8,128)(2,1)S(1)} %pad_maximum_fusion.1), channel_id=1, source_target_pairs={{0,6},{2,8},{4,10},{6,12},{8,14},{10,16},{12,18},{14,20},{16,22},{... | collective-permute-start | bytes 393224 | tf_op jit(solution)/shard_map/ppermute | solution.py:15
  40.5 3.4 %collective-permute-start = (bf16[2,256,1,128]{1,3,2,0:T(8,128)(2,1)S(1)}, bf16[2,256,1,128]{1,3,2,0:T(8,128)(2,1)S(1)}, u32[]{:S(2)}, u32[]{:S(2)}) collective-permute-start(bf16[2,256,1,128]{1,3,2,0:T(8,128)(2,1)S(1)} %pad_maximum_fusion.1), channel_id=1, source_target_pairs={{0,8},{2,10},{4,12},{6,14},{8,16},{10,18},{12,20},{14,22},{16,24},... | collective-permute-start | bytes 393224 | tf_op jit(solution)/shard_map/ppermute | solution.py:15
  43.9 0.0 copy-start.15
  43.9 0.6 multiply_reduce_fusion.1
  44.5 0.0 copy-done.15
  44.6 0.1 multiply_multiply_fusion
  44.7 0.6 fusion.21
  45.2 0.0 copy-start.10
  45.3 1.1 %collective-permute-done = bf16[2,256,1,128]{1,3,2,0:T(8,128)(2,1)S(1)} collective-permute-done((bf16[2,256,1,128]{1,3,2,0:T(8,128)(2,1)S(1)}, bf16[2,256,1,128]{1,3,2,0:T(8,128)(2,1)S(1)}, u32[]{:S(2)}, u32[]{:S(2)}) %collective-permute-start) | collective-permute-done | bytes 131104 | tf_op jit(solution)/shard_map/ppermute | solution.py:15
  46.5 0.8 fusion.73
  47.3 0.3 fusion.31
  47.6 0.5 convolution_bitcast_fusion.1
  48.1 0.3 fusion.25
  48.5 0.1 fusion.36
  48.5 0.6 fusion.8
  49.1 0.3 convolution_bitcast_fusion.3
  49.5 0.6 convolution_bitcast_fusion.2
  50.0 0.0 copy-start.5
  50.0 0.1 slice_bitcast_fusion.4
  50.1 0.1 maximum_convert_fusion
  50.2 0.8 fusion.72
  51.0 1.7 %convolution_convert_fusion = bf16[256,2688]{1,0:T(8,128)(2,1)} fusion(bf16[256,256]{0,1:T(8,128)(2,1)S(1)} %bitcast.160, bf16[256,2688]{1,0:T(8,128)(2,1)S(1)} %copy-done), kind=kOutput, calls=%fused_computation.3 | convolution fusion | flops 353009664 | bytes 2883584 | tf_op jit(solution)/shard_map/dot_general | solution.py:163
  52.7 0.0 reduce-scatter.3.cloned.1.call-update
  52.7 0.0 reduce-scatter.5.cloned.1.call-start
  52.8 1.3 %collective-permute-start.4 = (bf16[2,256,1,128]{1,3,2,0:T(8,128)(2,1)}, bf16[2,256,1,128]{1,3,2,0:T(8,128)(2,1)S(1)}, u32[]{:S(2)}, u32[]{:S(2)}) collective-permute-start(bf16[2,256,1,128]{1,3,2,0:T(8,128)(2,1)} %get-tuple-element.2), channel_id=1, source_target_pairs={{2,0},{4,2},{6,4},{8,6},{10,8},{12,10},{14,12},{16,14},{18,16},{20... | collective-permute-start | bytes 393224 | tf_op jit(solution)/shard_map/ppermute | solution.py:15
  54.1 1.3 %collective-permute-start.7 = (bf16[2,256,1,128]{1,3,2,0:T(8,128)(2,1)}, bf16[2,256,1,128]{1,3,2,0:T(8,128)(2,1)S(1)}, u32[]{:S(2)}, u32[]{:S(2)}) collective-permute-start(bf16[2,256,1,128]{1,3,2,0:T(8,128)(2,1)} %get-tuple-element.3), channel_id=1, source_target_pairs={{8,0},{10,2},{12,4},{14,6},{16,8},{18,10},{20,12},{22,14},{24,16},... | collective-permute-start | bytes 393224 | tf_op jit(solution)/shard_map/ppermute | solution.py:15
  55.4 1.3 %collective-permute-start.6 = (bf16[2,256,1,128]{1,3,2,0:T(8,128)(2,1)}, bf16[2,256,1,128]{1,3,2,0:T(8,128)(2,1)S(1)}, u32[]{:S(2)}, u32[]{:S(2)}) collective-permute-start(bf16[2,256,1,128]{1,3,2,0:T(8,128)(2,1)} %get-tuple-element.4), channel_id=1, source_target_pairs={{6,0},{8,2},{10,4},{12,6},{14,8},{16,10},{18,12},{20,14},{22,16},{... | collective-permute-start | bytes 393224 | tf_op jit(solution)/shard_map/ppermute | solution.py:15
  56.7 1.3 %collective-permute-start.5 = (bf16[2,256,1,128]{1,3,2,0:T(8,128)(2,1)}, bf16[2,256,1,128]{1,3,2,0:T(8,128)(2,1)S(1)}, u32[]{:S(2)}, u32[]{:S(2)}) collective-permute-start(bf16[2,256,1,128]{1,3,2,0:T(8,128)(2,1)} %get-tuple-element.5), channel_id=1, source_target_pairs={{4,0},{6,2},{8,4},{10,6},{12,8},{14,10},{16,12},{18,14},{20,16},{2... | collective-permute-start | bytes 393224 | tf_op jit(solution)/shard_map/ppermute | solution.py:15
  58.0 0.8 multiply_reduce_fusion
  58.8 0.8 fusion.35
  59.6 0.6 fusion.74
  60.2 0.0 copy-start.7
  60.2 4.8 %collective-permute-done.7 = bf16[2,256,1,128]{1,3,2,0:T(8,128)(2,1)S(1)} collective-permute-done((bf16[2,256,1,128]{1,3,2,0:T(8,128)(2,1)}, bf16[2,256,1,128]{1,3,2,0:T(8,128)(2,1)S(1)}, u32[]{:S(2)}, u32[]{:S(2)}) %collective-permute-start.7) | collective-permute-done | bytes 131104 | tf_op jit(solution)/shard_map/ppermute | solution.py:15
  65.0 1.3 %collective-permute-done.5 = bf16[2,256,1,128]{1,3,2,0:T(8,128)(2,1)S(1)} collective-permute-done((bf16[2,256,1,128]{1,3,2,0:T(8,128)(2,1)}, bf16[2,256,1,128]{1,3,2,0:T(8,128)(2,1)S(1)}, u32[]{:S(2)}, u32[]{:S(2)}) %collective-permute-start.5) | collective-permute-done | bytes 131104 | tf_op jit(solution)/shard_map/ppermute | solution.py:15
  66.3 0.1 convert_add_fusion
  66.4 0.9 %fusion.40 = f32[256,1,128]{0,2,1:T(8,128)S(1)} fusion(f32[2,256,1,128]{1,3,2,0:T(8,128)S(1)} %convert_add_fusion, f32[1280,1,128]{0,2,1:T(8,128)} %copy-done.5), kind=kLoop, calls=%fused_computation.66 | loop fusion | flops 32768 | bytes 393216 | tf_op jit(solution)/shard_map/add | solution.py:147
  67.3 0.3 fusion.54
  67.7 0.1 fusion.41
  67.8 0.6 convolution_add_fusion.1
  68.5 0.5 copy-done.9
  68.9 2.5 %fusion = bf16[256,2688]{1,0:T(8,128)(2,1)} fusion(f32[256,2688]{1,0:T(8,128)S(1)} %convolution_add_fusion.1, bf16[2688,128]{1,0:T(8,128)(2,1)S(1)} %copy-done.9, f32[2,256,1,128]{1,3,2,0:T(8,128)S(1)} %convert_add_fusion, f32[1280,1,128]{0,2,1:T(8,128)} %copy-done.4), kind=kOutput, calls=%fused_computation.2 | convolution fusion | flops 177602560 | bytes 5079040 | tf_op jit(solution)/shard_map/nh,dh->nd/dot_general | solution.py:171
  71.5 0.0 reduce-scatter.5.cloned.1.call-update
  71.5 0.0 reduce-scatter.3.cloned.1.call-done
  71.5 1.0 %copy-done.2 = bf16[128,2688]{1,0:T(8,128)(2,1)S(1)} copy-done((bf16[128,2688]{1,0:T(8,128)(2,1)S(1)}, bf16[128,2688]{1,0:T(8,128)(2,1)}, u32[]{:S(2)}) %copy-start.2) | copy-done | bytes 688152
  72.6 2.1 %add_convert_fusion.1 = bf16[128,2688]{1,0:T(8,128)(2,1)} fusion(bf16[128,2688]{1,0:T(8,128)(2,1)} %reduce-scatter.3.cloned.1.call-done, bf16[128,2688]{1,0:T(8,128)(2,1)S(1)} %copy-done.2), kind=kLoop, calls=%fused_computation.28 | loop fusion | flops 1376256 | bytes 2064384 | tf_op jit(solution)/shard_map/convert_element_type | solution.py:182
  74.7 8.9 %reduce-scatter.5.cloned.1.call-done = bf16[128,2688]{1,0:T(8,128)(2,1)} async-done(((bf16[256,2688]{1,0:T(8,128)(2,1)}), bf16[128,2688]{1,0:T(8,128)(2,1)}) %reduce-scatter.5.cloned.1.call-update) | async-done | bytes 688144 | tf_op jit(solution)/shard_map/reduce_scatter | solution.py:178
  83.6 2.1 %add_convert_fusion = bf16[128,2688]{1,0:T(8,128)(2,1)} fusion(bf16[128,2688]{1,0:T(8,128)(2,1)} %reduce-scatter.5.cloned.1.call-done, bf16[128,2688]{1,0:T(8,128)(2,1)S(1)} %copy-done.3), kind=kLoop, calls=%fused_computation.27 | loop fusion | flops 1376256 | bytes 2064384 | tf_op jit(solution)/shard_map/convert_element_type | solution.py:183
  (50 shorter events, 0.3 us)
Async XLA Ops:
  7.2 37.5 %copy-start = (bf16[256,2688]{1,0:T(8,128)(2,1)S(1)}, bf16[256,2688]{1,0:T(8,128)(2,1)}, u32[]{:S(2)}) copy-start(bf16[256,2688]{1,0:T(8,128)(2,1)} %param.13) | copy-start | bytes 4128772
  7.2 17.1 %all-gather.2.cloned.1.call-start = ((), (), s32[]{:S(2)}) async-start(), calls=%async_computation.2 | async-start | bytes 4128768 | tf_op jit(solution)/shard_map/all_gather | solution.py:89
  9.9 1.3 %copy-start.1 = (bf16[2688,256]{1,0:T(8,128)(2,1)S(1)}, bf16[2688,256]{1,0:T(8,128)(2,1)}, u32[]{:S(2)}) copy-start(bf16[2688,256]{1,0:T(8,128)(2,1)} %param.10) | copy-start | bytes 4128772
  9.9 61.6 %reduce-scatter.3.cloned.1.call-start = ((), (), s32[]{:S(2)}) async-start(), calls=%async_computation.3 | async-start | bytes 2064384 | tf_op jit(solution)/shard_map/reduce_scatter | solution.py:175
  12.9 13.9 %copy-start.13 = (f32[64]{0:T(128)}, f32[64]{0:T(128)S(1)}, u32[]{:S(2)}) copy-start(f32[64]{0:T(128)S(1)} %negate_power_fusion) | copy-start | bytes 772
  12.9 13.7 %copy-start.11 = (f32[128]{0:T(128)S(1)}, f32[128]{0:T(128)}, u32[]{:S(2)}) copy-start(f32[128]{0:T(128)} %param.15) | copy-start | bytes 1540
  24.3 2.8 %copy-start.8 = (bf16[2688,128]{1,0:T(8,128)(2,1)S(1)}, bf16[2688,128]{1,0:T(8,128)(2,1)}, u32[]{:S(2)}) copy-start(bf16[2688,128]{1,0:T(8,128)(2,1)} %param.12) | copy-start | bytes 2064388
  24.3 19.6 %copy-start.18 = (bf16[2,256,2688]{2,1,0:T(8,128)(2,1)S(1)}, bf16[2,256,2688]{2,1,0:T(8,128)(2,1)}, u32[]{:S(2)}) copy-start(bf16[2,256,2688]{2,1,0:T(8,128)(2,1)} %all-gather.2.cloned.1.call-done) | copy-start | bytes 8257540
  26.6 2.5 %copy-start.16 = (f32[256]{0:T(256)}, f32[256]{0:T(256)S(1)}, u32[]{:S(2)}) copy-start(f32[256]{0:T(256)S(1)} %get-tuple-element.18) | copy-start | bytes 3076
  26.7 17.1 %copy-start.6 = (bf16[256,2688]{1,0:T(8,128)(2,1)S(1)}, bf16[256,2688]{1,0:T(8,128)(2,1)}, u32[]{:S(2)}) copy-start(bf16[256,2688]{1,0:T(8,128)(2,1)} %copy.30) | copy-start | bytes 4128772
  29.1 17.3 %collective-permute-start.3 = (bf16[2,256,1,128]{1,3,2,0:T(8,128)(2,1)S(1)}, bf16[2,256,1,128]{1,3,2,0:T(8,128)(2,1)S(1)}, u32[]{:S(2)}, u32[]{:S(2)}) collective-permute-start(bf16[2,256,1,128]{1,3,2,0:T(8,128)(2,1)S(1)} %pad_maximum_fusion.1), channel_id=1, source_target_pairs={{0,2},{2,4},{4,6},{6,8},{8,10},{10,12},{12,14},{14,16},{16,18},{18... | collective-permute-start | bytes 393224 | tf_op jit(solution)/shard_map/ppermute | solution.py:15
  32.8 13.6 %collective-permute-start.2 = (bf16[2,256,1,128]{1,3,2,0:T(8,128)(2,1)S(1)}, bf16[2,256,1,128]{1,3,2,0:T(8,128)(2,1)S(1)}, u32[]{:S(2)}, u32[]{:S(2)}) collective-permute-start(bf16[2,256,1,128]{1,3,2,0:T(8,128)(2,1)S(1)} %pad_maximum_fusion.1), channel_id=1, source_target_pairs={{0,4},{2,6},{4,8},{6,10},{8,12},{10,14},{12,16},{14,18},{16,20},{1... | collective-permute-start | bytes 393224 | tf_op jit(solution)/shard_map/ppermute | solution.py:15
  36.2 10.2 %collective-permute-start.1 = (bf16[2,256,1,128]{1,3,2,0:T(8,128)(2,1)S(1)}, bf16[2,256,1,128]{1,3,2,0:T(8,128)(2,1)S(1)}, u32[]{:S(2)}, u32[]{:S(2)}) collective-permute-start(bf16[2,256,1,128]{1,3,2,0:T(8,128)(2,1)S(1)} %pad_maximum_fusion.1), channel_id=1, source_target_pairs={{0,6},{2,8},{4,10},{6,12},{8,14},{10,16},{12,18},{14,20},{16,22},{... | collective-permute-start | bytes 393224 | tf_op jit(solution)/shard_map/ppermute | solution.py:15
  40.5 5.9 %collective-permute-start = (bf16[2,256,1,128]{1,3,2,0:T(8,128)(2,1)S(1)}, bf16[2,256,1,128]{1,3,2,0:T(8,128)(2,1)S(1)}, u32[]{:S(2)}, u32[]{:S(2)}) collective-permute-start(bf16[2,256,1,128]{1,3,2,0:T(8,128)(2,1)S(1)} %pad_maximum_fusion.1), channel_id=1, source_target_pairs={{0,8},{2,10},{4,12},{6,14},{8,16},{10,18},{12,20},{14,22},{16,24},... | collective-permute-start | bytes 393224 | tf_op jit(solution)/shard_map/ppermute | solution.py:15
  43.9 0.7 copy-start.15
  45.2 1.3 %copy-start.10 = (pred[256,1280]{0,1:T(8,128)(4,1)S(1)}, pred[256,1280]{0,1:T(8,128)(4,1)}, u32[]{:S(2)}) copy-start(pred[256,1280]{0,1:T(8,128)(4,1)} %fusion.20) | copy-start | bytes 983044
  48.1 1.9 %copy-start.4 = (f32[1280,1,128]{0,2,1:T(8,128)}, f32[1280,1,128]{0,2,1:T(8,128)S(1)}, u32[]{:S(2)}) copy-start(f32[1280,1,128]{0,2,1:T(8,128)S(1)} %convolution_bitcast_fusion.1) | copy-start | bytes 1966084
  50.0 1.0 %copy-start.5 = (f32[1280,1,128]{0,2,1:T(8,128)}, f32[1280,1,128]{0,2,1:T(8,128)S(1)}, u32[]{:S(2)}) copy-start(f32[1280,1,128]{0,2,1:T(8,128)S(1)} %convolution_bitcast_fusion.2) | copy-start | bytes 1966084
  52.7 30.9 %reduce-scatter.5.cloned.1.call-start = ((), (), s32[]{:S(2)}) async-start(), calls=%async_computation.4 | async-start | bytes 2064384 | tf_op jit(solution)/shard_map/reduce_scatter | solution.py:178
  52.8 7.4 %collective-permute-start.4 = (bf16[2,256,1,128]{1,3,2,0:T(8,128)(2,1)}, bf16[2,256,1,128]{1,3,2,0:T(8,128)(2,1)S(1)}, u32[]{:S(2)}, u32[]{:S(2)}) collective-permute-start(bf16[2,256,1,128]{1,3,2,0:T(8,128)(2,1)} %get-tuple-element.2), channel_id=1, source_target_pairs={{2,0},{4,2},{6,4},{8,6},{10,8},{12,10},{14,12},{16,14},{18,16},{20... | collective-permute-start | bytes 393224 | tf_op jit(solution)/shard_map/ppermute | solution.py:15
  54.1 10.9 %collective-permute-start.7 = (bf16[2,256,1,128]{1,3,2,0:T(8,128)(2,1)}, bf16[2,256,1,128]{1,3,2,0:T(8,128)(2,1)S(1)}, u32[]{:S(2)}, u32[]{:S(2)}) collective-permute-start(bf16[2,256,1,128]{1,3,2,0:T(8,128)(2,1)} %get-tuple-element.3), channel_id=1, source_target_pairs={{8,0},{10,2},{12,4},{14,6},{16,8},{18,10},{20,12},{22,14},{24,16},... | collective-permute-start | bytes 393224 | tf_op jit(solution)/shard_map/ppermute | solution.py:15
  55.4 9.6 %collective-permute-start.6 = (bf16[2,256,1,128]{1,3,2,0:T(8,128)(2,1)}, bf16[2,256,1,128]{1,3,2,0:T(8,128)(2,1)S(1)}, u32[]{:S(2)}, u32[]{:S(2)}) collective-permute-start(bf16[2,256,1,128]{1,3,2,0:T(8,128)(2,1)} %get-tuple-element.4), channel_id=1, source_target_pairs={{6,0},{8,2},{10,4},{12,6},{14,8},{16,10},{18,12},{20,14},{22,16},{... | collective-permute-start | bytes 393224 | tf_op jit(solution)/shard_map/ppermute | solution.py:15
  56.7 9.6 %collective-permute-start.5 = (bf16[2,256,1,128]{1,3,2,0:T(8,128)(2,1)}, bf16[2,256,1,128]{1,3,2,0:T(8,128)(2,1)S(1)}, u32[]{:S(2)}, u32[]{:S(2)}) collective-permute-start(bf16[2,256,1,128]{1,3,2,0:T(8,128)(2,1)} %get-tuple-element.5), channel_id=1, source_target_pairs={{4,0},{6,2},{8,4},{10,6},{12,8},{14,10},{16,12},{18,14},{20,16},{2... | collective-permute-start | bytes 393224 | tf_op jit(solution)/shard_map/ppermute | solution.py:15
  59.6 7.7 %copy-start.14 = (f32[64]{0:T(128)S(1)}, f32[64]{0:T(128)}, u32[]{:S(2)}) copy-start(f32[64]{0:T(128)} %copy-done.13) | copy-start | bytes 772
  60.2 7.5 %copy-start.12 = (f32[128]{0:T(128)S(1)}, f32[128]{0:T(128)}, u32[]{:S(2)}) copy-start(f32[128]{0:T(128)} %param.15) | copy-start | bytes 1540
  60.2 7.6 %copy-start.17 = (f32[256]{0:T(256)S(1)}, f32[256]{0:T(256)}, u32[]{:S(2)}) copy-start(f32[256]{0:T(256)} %copy-done.16) | copy-start | bytes 3076
  60.2 7.6 %copy-start.7 = (bf16[2688,128]{1,0:T(8,128)(2,1)S(1)}, bf16[2688,128]{1,0:T(8,128)(2,1)}, u32[]{:S(2)}) copy-start(bf16[2688,128]{1,0:T(8,128)(2,1)} %param.11) | copy-start | bytes 2064388
  67.8 1.1 %copy-start.9 = (bf16[2688,128]{1,0:T(8,128)(2,1)S(1)}, bf16[2688,128]{1,0:T(8,128)(2,1)}, u32[]{:S(2)}) copy-start(bf16[2688,128]{1,0:T(8,128)(2,1)} %param.12) | copy-start | bytes 2064388
  71.5 1.1 %copy-start.2 = (bf16[128,2688]{1,0:T(8,128)(2,1)S(1)}, bf16[128,2688]{1,0:T(8,128)(2,1)}, u32[]{:S(2)}) copy-start(bf16[128,2688]{1,0:T(8,128)(2,1)} %param.8) | copy-start | bytes 2064388
  71.5 12.1 %copy-start.3 = (bf16[128,2688]{1,0:T(8,128)(2,1)S(1)}, bf16[128,2688]{1,0:T(8,128)(2,1)}, u32[]{:S(2)}) copy-start(bf16[128,2688]{1,0:T(8,128)(2,1)} %param.9) | copy-start | bytes 2064388
Sparse Core Ops, SparseCore 0:
  10.0 14.2 all-gather.1
  52.8 8.9 reduce-scatter.2
  71.6 11.9 reduce-scatter.4
where the time goes:
time: 92.8 us; the launch traced here: 92.2 us
  waiting for transfers between devices  25.6 us (28%)
  starting transfers between devices  20 us (22%)
  between operations  14.3 us (15%)
  matrix products  14 us (15%)
  other arithmetic  12.8 us (14%)
  local copies, waits for them, and re-layouts  5.53 us (6%)
    ppermute x8, starting transfers between devices, from_behind(): return lax.ppermute(block, axis, route)  19.9 us
    all_gather x1, waiting for transfers between devices, on_device(): portion = lax.all_gather(stacked, 'tp', axis=1, tiled=True)  9.45 us
    reduce_scatter x1, waiting for transfers between devices, on_device(): lax.psum_scatter(summed.astype(jnp.bfloat16), 'tp', scatter_dimension=0,...  8.92 us
    ppermute x8, waiting for transfers between devices, from_behind(): return lax.ppermute(block, axis, route)  7.18 us
    unnamed x41, local copies, waits for them, and re-layouts  2.91 us
    another operation x1, other arithmetic, on_device(): stacked = jnp.stack([tokens, result_grad])  2.66 us
    dot_general x1, matrix products, on_device(): jnp.einsum('nh,dh->nd', value_rows, value_weight, preferred_element_type=...  2.54 us
    dot_general x1, matrix products, on_device(): jnp.dot(inputs_part, key_weight, preferred_element_type=jnp.float32)  2.28 us
  transfers between devices with their start and end apart: 11, of which 5 were waited for; matrix products, arithmetic and copies ran while one was open for 15% of the time, Pallas kernels for 0%

commit v1 on v0

--- a/solution.py
+++ b/solution.py
@@ -86,7 +86,7 @@
     kv_count = kv_cols // head_size
     per_kv = query_cols // kv_cols
     stacked = jnp.stack([tokens, result_grad])
-    portion = lax.all_gather(stacked, "tp", axis=1, tiled=True)
+    portion = jnp.concatenate(lax.all_gather(stacked, "tp"), axis=1)
     inputs_part = portion[0]
     gradients_part = portion[1]
     query_rows = jnp.dot(inputs_part, query_weight, preferred_element_type=jnp.float32)

time: 92.8 us -> 98.8 us (1.065)
  waiting for transfers between devices: 25.6 us -> 29.1 us
  other arithmetic: 12.8 us -> 16 us
  local copies, waits for them, and re-layouts: 5.53 us -> 7.9 us
  matrix products: 14 us -> 11.7 us
    all_gather x0 -> x1, local copies, waits for them, and re-layouts: none -> 1.99 us  [on_device(): portion = jnp.concatenate(lax.all_gather(stacked, 'tp'), axis=1)]
    dot_general x1, matrix products: 2.28 us -> 0.62 us  [on_device(): jnp.dot(inputs_part, key_weight, preferred_element_type=jnp.float32)]
    ppermute x8, waiting for transfers between devices: 7.18 us -> 8.61 us  [from_behind(): return lax.ppermute(block, axis, route)]
    dot_general x1, matrix products: 2.01 us -> 0.61 us  [on_device(): jnp.dot(inputs_part, value_weight, preferred_element_type=jnp.float32)]
    reduce_scatter x1, waiting for transfers between devices: 0.02 us -> 1.38 us  [on_device(): lax.psum_scatter(out_part.astype(jnp.bfloat16), 'tp', scatter_dimension=0...]
    reduce_scatter x1, waiting for transfers between devices: 8.92 us -> 10.2 us  [on_device(): lax.psum_scatter(summed.astype(jnp.bfloat16), 'tp', scatter_dimension=0,...]
    add x1, other arithmetic: 0.07 us -> 1.16 us  [on_device(): returned = returned + arrived]
    unnamed x41 -> x37, local copies, waits for them, and re-layouts: 2.91 us -> 3.08 us
  transfers between devices with their start and end apart: 11 -> 11, of which waited for: 5 -> 7; matrix products, arithmetic and copies ran while one was open for 15% -> 19% of each run, Pallas kernels for 0% -> 0%
where the time goes in v1:
time: 98.8 us; the launch traced here: 98.1 us
  waiting for transfers between devices  29.1 us (29%)
  starting transfers between devices  19.1 us (19%)
  other arithmetic  16 us (16%)
  between operations  14.2 us (14%)
  matrix products  11.7 us (12%)
  local copies, waits for them, and re-layouts  7.9 us (8%)
    ppermute x8, starting transfers between devices, from_behind(): return lax.ppermute(block, axis, route)  19 us
    reduce_scatter x1, waiting for transfers between devices, on_device(): lax.psum_scatter(summed.astype(jnp.bfloat16), 'tp', scatter_dimension=0,...  10.2 us
    all_gather x1, waiting for transfers between devices, on_device(): portion = jnp.concatenate(lax.all_gather(stacked, 'tp'), axis=1)  8.87 us
    ppermute x8, waiting for transfers between devices, from_behind(): return lax.ppermute(block, axis, route)  8.61 us
    unnamed x37, local copies, waits for them, and re-layouts  3.08 us
    another operation x1, other arithmetic, on_device(): stacked = jnp.stack([tokens, result_grad])  2.66 us
    dot_general x1, matrix products, on_device(): jnp.einsum('nh,dh->nd', value_rows, value_weight, preferred_element_type=...  2.56 us
    convert_element_type x1, other arithmetic, on_device(): layer_output = (tokens.astype(jnp.float32) + out_sum).astype(jnp.bfloat16)  2.1 us
  transfers between devices with their start and end apart: 11, of which 7 were waited for; matrix products, arithmetic and copies ran while one was open for 19% of the time, Pallas kernels for 0%

profile of v1, /device:TPU:0, one launch (start us, length us, event | category | flops | bytes accessed | tf_op | source)
XLA Modules:
  0.0 98.1 jit_solution(714439358830853837)
XLA Ops:
  7.2 0.0 all-gather.3.cloned.1.call-start
  7.2 2.7 %pad_maximum_fusion = bf16[2,128,2688]{2,1,0:T(8,128)(2,1)} fusion(bf16[1,128,2688]{2,1,0:T(8,128)(2,1)} %bitcast.156, bf16[1,128,2688]{2,1,0:T(8,128)(2,1)} %bitcast.155), kind=kLoop, calls=%fused_computation.19 | loop fusion | flops 688128 | bytes 2752512 | tf_op jit(solution)/shard_map/stack | solution.py:88
  9.9 0.0 all-gather.3.cloned.1.call-update
  9.9 0.0 reduce-scatter.3.cloned.1.call-start
  10.0 1.3 %copy-done.1 = bf16[2688,256]{1,0:T(8,128)(2,1)S(1)} copy-done((bf16[2688,256]{1,0:T(8,128)(2,1)S(1)}, bf16[2688,256]{1,0:T(8,128)(2,1)}, u32[]{:S(2)}) %copy-start.1) | copy-done | bytes 1376280
  11.2 1.7 %copy.42 = bf16[256,2688]{1,0:T(8,128)(2,1)} copy(bf16[256,2688]{0,1:T(8,128)(2,1)S(1)} %bitcast.153) | data formatting | bytes 2752512 | tf_op jit(solution)/shard_map/dot_general | solution.py:92
  12.9 0.9 multiply_cosine_fusion
  13.9 1.6 %fusion.13 = pred[256,1280]{0,1:T(8,128)(4,1)} fusion(s32[1280]{0:T(1024)S(1)} %iota_add_fusion, s32[256]{0:T(256)S(1)} %iota_add_fusion.1, pred[1280]{0:T(1024)(128)(4,1)S(1)} %broadcast_compare_fusion), kind=kLoop, calls=%fused_computation.27 | loop fusion | flops 1638400 | bytes 335104 | tf_op jit(solution)/shard_map/and | solution.py:53
  15.5 8.9 %all-gather.3.cloned.1.call-done = bf16[4,128,2688]{2,1,0:T(8,128)(2,1)} async-done(((bf16[2,128,2688]{2,1,0:T(8,128)(2,1)}), bf16[4,128,2688]{2,1,0:T(8,128)(2,1)}) %all-gather.3.cloned.1.call-update) | async-done | bytes 2752528 | tf_op jit(solution)/shard_map/all_gather | solution.py:89
  24.3 2.0 %copy.45 = bf16[2,2,128,2688]{3,2,0,1:T(8,128)(2,1)S(1)} copy(bf16[2,2,128,2688]{3,2,1,0:T(8,128)(2,1)} %bitcast.154) | data formatting | bytes 5505024 | tf_op jit(solution)/shard_map/all_gather | solution.py:89
  26.3 0.2 fusion.58
  26.6 0.8 copy-done.3
  27.4 0.6 multiply_reduce_fusion.2
  28.1 0.6 copy-done.8
  28.7 0.1 multiply_bitcast_fusion
  28.8 0.3 fusion.37
  29.1 0.6 convolution_convert_fusion.2
  29.8 3.7 %collective-permute-start = (bf16[2,256,1,128]{1,3,2,0:T(8,128)(2,1)S(1)}, bf16[2,256,1,128]{1,3,2,0:T(8,128)(2,1)S(1)}, u32[]{:S(2)}, u32[]{:S(2)}) collective-permute-start(bf16[2,256,1,128]{1,3,2,0:T(8,128)(2,1)S(1)} %pad_maximum_fusion.1), channel_id=1, source_target_pairs={{0,8},{2,10},{4,12},{6,14},{8,16},{10,18},{12,20},{14,22},{16,24},... | collective-permute-start | bytes 393224 | tf_op jit(solution)/shard_map/ppermute | solution.py:15
  33.4 4.3 %collective-permute-start.1 = (bf16[2,256,1,128]{1,3,2,0:T(8,128)(2,1)S(1)}, bf16[2,256,1,128]{1,3,2,0:T(8,128)(2,1)S(1)}, u32[]{:S(2)}, u32[]{:S(2)}) collective-permute-start(bf16[2,256,1,128]{1,3,2,0:T(8,128)(2,1)S(1)} %pad_maximum_fusion.1), channel_id=1, source_target_pairs={{0,6},{2,8},{4,10},{6,12},{8,14},{10,16},{12,18},{14,20},{16,22},{... | collective-permute-start | bytes 393224 | tf_op jit(solution)/shard_map/ppermute | solution.py:15
  37.7 3.4 %collective-permute-start.2 = (bf16[2,256,1,128]{1,3,2,0:T(8,128)(2,1)S(1)}, bf16[2,256,1,128]{1,3,2,0:T(8,128)(2,1)S(1)}, u32[]{:S(2)}, u32[]{:S(2)}) collective-permute-start(bf16[2,256,1,128]{1,3,2,0:T(8,128)(2,1)S(1)} %pad_maximum_fusion.1), channel_id=1, source_target_pairs={{0,4},{2,6},{4,8},{6,10},{8,12},{10,14},{12,16},{14,18},{16,20},{1... | collective-permute-start | bytes 393224 | tf_op jit(solution)/shard_map/ppermute | solution.py:15
  41.1 2.5 %collective-permute-start.3 = (bf16[2,256,1,128]{1,3,2,0:T(8,128)(2,1)S(1)}, bf16[2,256,1,128]{1,3,2,0:T(8,128)(2,1)S(1)}, u32[]{:S(2)}, u32[]{:S(2)}) collective-permute-start(bf16[2,256,1,128]{1,3,2,0:T(8,128)(2,1)S(1)} %pad_maximum_fusion.1), channel_id=1, source_target_pairs={{0,2},{2,4},{4,6},{6,8},{8,10},{10,12},{12,14},{14,16},{16,18},{18... | collective-permute-start | bytes 393224 | tf_op jit(solution)/shard_map/ppermute | solution.py:15
  43.6 0.6 multiply_reduce_fusion.1
  44.3 0.6 convolution_convert_fusion.1
  44.8 0.1 copy-done.7
  44.9 0.0 copy-done.16
  44.9 0.1 multiply_multiply_fusion
  45.0 0.1 copy-done.13
  45.3 0.8 collective-permute-done.3
  46.2 0.8 fusion.60
  46.9 0.3 fusion.20
  47.2 0.3 fusion.17
  47.5 0.6 convolution_bitcast_fusion.1
  48.1 0.1 fusion.22
  48.2 0.6 fusion.8
  48.8 0.6 convolution_bitcast_fusion.2
  49.3 1.1 %convolution_bitcast_fusion.3 = f32[256,2,128]{0,2,1:T(8,128)} fusion(bf16[2,256,1280]{1,2,0:T(8,128)(2,1)S(1)} %fusion.8, bf16[256,1,64]{0,2,1:T(8,128)(2,1)S(1)} %get-tuple-element.17, bf16[256,1,64]{0,2,1:T(8,128)(2,1)S(1)} %get-tuple-element.16, bf16[1024,1,128]{0,2,1:T(8,128)(2,1)S(1)} %get-tuple-element.9), kind=kOutput, calls=%fused_computation.28 | convolution fusion | flops 168755200 | bytes 1900544 | tf_op jit(solution)/shard_map/kgqc,ckh->qkgh/dot_general | solution.py:68
  50.4 0.1 slice_bitcast_fusion
  50.5 0.1 maximum_convert_fusion
  50.6 0.8 fusion.59
  51.4 1.3 %collective-permute-start.4 = (bf16[2,256,1,128]{1,3,2,0:T(8,128)(2,1)}, bf16[2,256,1,128]{1,3,2,0:T(8,128)(2,1)}, u32[]{:S(2)}, u32[]{:S(2)}) collective-permute-start(bf16[2,256,1,128]{1,3,2,0:T(8,128)(2,1)} %get-tuple-element.4), channel_id=1, source_target_pairs={{2,0},{4,2},{6,4},{8,6},{10,8},{12,10},{14,12},{16,14},{18,16},{20... | collective-permute-start | bytes 393224 | tf_op jit(solution)/shard_map/ppermute | solution.py:15
  52.7 1.3 %collective-permute-start.5 = (bf16[2,256,1,128]{1,3,2,0:T(8,128)(2,1)}, bf16[2,256,1,128]{1,3,2,0:T(8,128)(2,1)}, u32[]{:S(2)}, u32[]{:S(2)}) collective-permute-start(bf16[2,256,1,128]{1,3,2,0:T(8,128)(2,1)} %get-tuple-element.7), channel_id=1, source_target_pairs={{4,0},{6,2},{8,4},{10,6},{12,8},{14,10},{16,12},{18,14},{20,16},{2... | collective-permute-start | bytes 393224 | tf_op jit(solution)/shard_map/ppermute | solution.py:15
  54.0 1.3 %collective-permute-start.6 = (bf16[2,256,1,128]{1,3,2,0:T(8,128)(2,1)}, bf16[2,256,1,128]{1,3,2,0:T(8,128)(2,1)}, u32[]{:S(2)}, u32[]{:S(2)}) collective-permute-start(bf16[2,256,1,128]{1,3,2,0:T(8,128)(2,1)} %get-tuple-element.6), channel_id=1, source_target_pairs={{6,0},{8,2},{10,4},{12,6},{14,8},{16,10},{18,12},{20,14},{22,16},{... | collective-permute-start | bytes 393224 | tf_op jit(solution)/shard_map/ppermute | solution.py:15
  55.3 1.3 %collective-permute-start.7 = (bf16[2,256,1,128]{1,3,2,0:T(8,128)(2,1)}, bf16[2,256,1,128]{1,3,2,0:T(8,128)(2,1)}, u32[]{:S(2)}, u32[]{:S(2)}) collective-permute-start(bf16[2,256,1,128]{1,3,2,0:T(8,128)(2,1)} %get-tuple-element.5), channel_id=1, source_target_pairs={{8,0},{10,2},{12,4},{14,6},{16,8},{18,10},{20,12},{22,14},{24,16},... | collective-permute-start | bytes 393224 | tf_op jit(solution)/shard_map/ppermute | solution.py:15
  56.6 1.7 %convolution_convert_fusion = bf16[256,2688]{1,0:T(8,128)(2,1)} fusion(bf16[256,256]{0,1:T(8,128)(2,1)S(1)} %bitcast.159, bf16[256,2688]{1,0:T(8,128)(2,1)S(1)} %copy-done), kind=kOutput, calls=%fused_computation.3 | convolution fusion | flops 353009664 | bytes 2883584 | tf_op jit(solution)/shard_map/dot_general | solution.py:163
  58.3 0.0 reduce-scatter.3.cloned.1.call-update
  58.3 0.0 reduce-scatter.5.cloned.1.call-start
  58.3 1.0 %multiply_add_fusion.1 = (f32[256,2,64]{0,2,1:T(8,128)S(1)}, f32[256,2,64]{0,2,1:T(8,128)S(1)}) fusion(f32[256,2,128]{0,2,1:T(8,128)} %convolution_bitcast_fusion.3, f32[256,64]{0,1:T(8,128)} %get-tuple-element.19, f32[256,64]{0,1:T(8,128)S(1)} %get-tuple-element.18), kind=kLoop, calls=%fused_computation.63 | loop fusion | flops 229376 | bytes 655360 | tf_op jit(solution)/shard_map/transpose(jvp())/add_any | solution.py:38
  59.4 1.1 %multiply_reduce_fusion = f32[256,2]{0,1:T(2,128)S(1)} fusion(f32[256,2,128]{0,2,1:T(8,128)} %copy-done.7, f32[256,2,64]{0,2,1:T(8,128)S(1)} %get-tuple-element.11, f32[256,2,64]{0,2,1:T(8,128)S(1)} %get-tuple-element.10, f32[128]{0:T(128)S(1)} %copy-done.16), kind=kLoop, calls=%fused_computation.46 | loop fusion | flops 261632 | bytes 526848 | tf_op jit(solution)/shard_map/transpose(jvp())/reduce_sum | solution.py:31
  60.4 1.1 %fusion.21 = bf16[256,2,128]{0,2,1:T(8,128)(2,1)S(1)} fusion(f32[256,2,128]{0,2,1:T(8,128)} %copy-done.7, f32[256,2,64]{0,2,1:T(8,128)S(1)} %get-tuple-element.11, f32[256,2,64]{0,2,1:T(8,128)S(1)} %get-tuple-element.10, f32[256,2]{0,1:T(2,128)S(1)} %multiply_multiply_fusion.1, f32[128]{0:T(128)S(1)} %copy-done.16, f32[256,2]{0,1:T(2,128)S(1)} %fusion.49), kind=kLoop, calls=%fused_computation.40 | loop fusion | flops 458752 | bytes 659968 | tf_op jit(solution)/shard_map/convert_element_type | solution.py:160
  61.5 0.6 fusion.61
  62.1 2.0 %collective-permute-done.5 = bf16[2,256,1,128]{1,3,2,0:T(8,128)(2,1)} collective-permute-done((bf16[2,256,1,128]{1,3,2,0:T(8,128)(2,1)}, bf16[2,256,1,128]{1,3,2,0:T(8,128)(2,1)}, u32[]{:S(2)}, u32[]{:S(2)}) %collective-permute-start.5) | collective-permute-done | bytes 131104 | tf_op jit(solution)/shard_map/ppermute | solution.py:15
  64.2 2.0 %collective-permute-done.6 = bf16[2,256,1,128]{1,3,2,0:T(8,128)(2,1)} collective-permute-done((bf16[2,256,1,128]{1,3,2,0:T(8,128)(2,1)}, bf16[2,256,1,128]{1,3,2,0:T(8,128)(2,1)}, u32[]{:S(2)}, u32[]{:S(2)}) %collective-permute-start.6) | collective-permute-done | bytes 131104 | tf_op jit(solution)/shard_map/ppermute | solution.py:15
  66.1 3.8 %collective-permute-done.7 = bf16[2,256,1,128]{1,3,2,0:T(8,128)(2,1)} collective-permute-done((bf16[2,256,1,128]{1,3,2,0:T(8,128)(2,1)}, bf16[2,256,1,128]{1,3,2,0:T(8,128)(2,1)}, u32[]{:S(2)}, u32[]{:S(2)}) %collective-permute-start.7) | collective-permute-done | bytes 131104 | tf_op jit(solution)/shard_map/ppermute | solution.py:15
  69.9 1.2 %convert_add_fusion = f32[2,256,1,128]{1,3,2,0:T(8,128)S(1)} fusion(bf16[2,256,1,128]{1,3,2,0:T(8,128)(2,1)} %collective-permute-done.7, bf16[2,256,1,128]{1,3,2,0:T(8,128)(2,1)} %collective-permute-done.6, bf16[2,256,1,128]{1,3,2,0:T(8,128)(2,1)} %collective-permute-done.5, bf16[2,256,1,128]{1,3,2,0:T(8,128)(2,1)} %collective-permute-done.4), kind=kLoop, calls=%fused_computation.45 | loop fusion | flops 458752 | bytes 786432 | tf_op jit(solution)/shard_map/add | solution.py:143
  71.1 0.9 fusion.26
  72.0 0.3 fusion.40
  72.4 0.1 fusion.27
  72.5 0.6 convolution_add_fusion.1
  73.1 2.6 %fusion = bf16[256,2688]{1,0:T(8,128)(2,1)} fusion(f32[256,2688]{1,0:T(8,128)S(1)} %convolution_add_fusion.1, bf16[2688,128]{1,0:T(8,128)(2,1)S(1)} %copy-done.2, f32[2,256,1,128]{1,3,2,0:T(8,128)S(1)} %convert_add_fusion, f32[1280,1,128]{0,2,1:T(8,128)} %copy-done.10), kind=kOutput, calls=%fused_computation.2 | convolution fusion | flops 177602560 | bytes 5079040 | tf_op jit(solution)/shard_map/nh,dh->nd/dot_general | solution.py:171
  75.7 0.0 reduce-scatter.5.cloned.1.call-update
  75.7 1.4 %reduce-scatter.3.cloned.1.call-done = bf16[128,2688]{1,0:T(8,128)(2,1)} async-done(((bf16[256,2688]{1,0:T(8,128)(2,1)}), bf16[128,2688]{1,0:T(8,128)(2,1)}) %reduce-scatter.3.cloned.1.call-update) | async-done | bytes 688144 | tf_op jit(solution)/shard_map/reduce_scatter | solution.py:175
  77.1 2.1 %add_convert_fusion.1 = bf16[128,2688]{1,0:T(8,128)(2,1)} fusion(bf16[128,2688]{1,0:T(8,128)(2,1)} %reduce-scatter.3.cloned.1.call-done, bf16[128,2688]{1,0:T(8,128)(2,1)S(1)} %copy-done.5), kind=kLoop, calls=%fused_computation.21 | loop fusion | flops 1376256 | bytes 2064384 | tf_op jit(solution)/shard_map/convert_element_type | solution.py:182
  79.2 10.2 %reduce-scatter.5.cloned.1.call-done = bf16[128,2688]{1,0:T(8,128)(2,1)} async-done(((bf16[256,2688]{1,0:T(8,128)(2,1)}), bf16[128,2688]{1,0:T(8,128)(2,1)}) %reduce-scatter.5.cloned.1.call-update) | async-done | bytes 688144 | tf_op jit(solution)/shard_map/reduce_scatter | solution.py:178
  89.5 2.1 %add_convert_fusion = bf16[128,2688]{1,0:T(8,128)(2,1)} fusion(bf16[128,2688]{1,0:T(8,128)(2,1)} %reduce-scatter.5.cloned.1.call-done, bf16[128,2688]{1,0:T(8,128)(2,1)S(1)} %copy-done.6), kind=kLoop, calls=%fused_computation.20 | loop fusion | flops 1376256 | bytes 2064384 | tf_op jit(solution)/shard_map/convert_element_type | solution.py:183
  (48 shorter events, 0.3 us)
Async XLA Ops:
  7.2 37.1 %copy-start = (bf16[256,2688]{1,0:T(8,128)(2,1)S(1)}, bf16[256,2688]{1,0:T(8,128)(2,1)}, u32[]{:S(2)}) copy-start(bf16[256,2688]{1,0:T(8,128)(2,1)} %param.13) | copy-start | bytes 4128772
  7.2 17.2 %all-gather.3.cloned.1.call-start = ((), (), s32[]{:S(2)}) async-start(), calls=%async_computation.4 | async-start | bytes 4128768 | tf_op jit(solution)/shard_map/all_gather | solution.py:89
  9.9 1.3 %copy-start.1 = (bf16[2688,256]{1,0:T(8,128)(2,1)S(1)}, bf16[2688,256]{1,0:T(8,128)(2,1)}, u32[]{:S(2)}) copy-start(bf16[2688,256]{1,0:T(8,128)(2,1)} %param.10) | copy-start | bytes 4128772
  9.9 67.2 %reduce-scatter.3.cloned.1.call-start = ((), (), s32[]{:S(2)}) async-start(), calls=%async_computation.2 | async-start | bytes 2064384 | tf_op jit(solution)/shard_map/reduce_scatter | solution.py:175
  26.3 1.1 %copy-start.3 = (bf16[2688,128]{1,0:T(8,128)(2,1)S(1)}, bf16[2688,128]{1,0:T(8,128)(2,1)}, u32[]{:S(2)}) copy-start(bf16[2688,128]{1,0:T(8,128)(2,1)} %param.11) | copy-start | bytes 2064388
  26.6 2.1 %copy-start.15 = (f32[128]{0:T(128)S(1)}, f32[128]{0:T(128)}, u32[]{:S(2)}) copy-start(f32[128]{0:T(128)} %param.15) | copy-start | bytes 1540
  26.6 2.6 %copy-start.2 = (bf16[2688,128]{1,0:T(8,128)(2,1)S(1)}, bf16[2688,128]{1,0:T(8,128)(2,1)}, u32[]{:S(2)}) copy-start(bf16[2688,128]{1,0:T(8,128)(2,1)} %param.12) | copy-start | bytes 2064388
  28.1 0.7 copy-start.8
  28.7 14.9 %copy-start.12 = (bf16[256,2688]{1,0:T(8,128)(2,1)S(1)}, bf16[256,2688]{1,0:T(8,128)(2,1)}, u32[]{:S(2)}) copy-start(bf16[256,2688]{1,0:T(8,128)(2,1)} %copy.42) | copy-start | bytes 4128772
  29.8 15.5 %collective-permute-start = (bf16[2,256,1,128]{1,3,2,0:T(8,128)(2,1)S(1)}, bf16[2,256,1,128]{1,3,2,0:T(8,128)(2,1)S(1)}, u32[]{:S(2)}, u32[]{:S(2)}) collective-permute-start(bf16[2,256,1,128]{1,3,2,0:T(8,128)(2,1)S(1)} %pad_maximum_fusion.1), channel_id=1, source_target_pairs={{0,8},{2,10},{4,12},{6,14},{8,16},{10,18},{12,20},{14,22},{16,24},... | collective-permute-start | bytes 393224 | tf_op jit(solution)/shard_map/ppermute | solution.py:15
  33.4 11.8 %collective-permute-start.1 = (bf16[2,256,1,128]{1,3,2,0:T(8,128)(2,1)S(1)}, bf16[2,256,1,128]{1,3,2,0:T(8,128)(2,1)S(1)}, u32[]{:S(2)}, u32[]{:S(2)}) collective-permute-start(bf16[2,256,1,128]{1,3,2,0:T(8,128)(2,1)S(1)} %pad_maximum_fusion.1), channel_id=1, source_target_pairs={{0,6},{2,8},{4,10},{6,12},{8,14},{10,16},{12,18},{14,20},{16,22},{... | collective-permute-start | bytes 393224 | tf_op jit(solution)/shard_map/ppermute | solution.py:15
  37.7 7.5 %collective-permute-start.2 = (bf16[2,256,1,128]{1,3,2,0:T(8,128)(2,1)S(1)}, bf16[2,256,1,128]{1,3,2,0:T(8,128)(2,1)S(1)}, u32[]{:S(2)}, u32[]{:S(2)}) collective-permute-start(bf16[2,256,1,128]{1,3,2,0:T(8,128)(2,1)S(1)} %pad_maximum_fusion.1), channel_id=1, source_target_pairs={{0,4},{2,6},{4,8},{6,10},{8,12},{10,14},{12,16},{14,18},{16,20},{1... | collective-permute-start | bytes 393224 | tf_op jit(solution)/shard_map/ppermute | solution.py:15
  41.1 5.0 %collective-permute-start.3 = (bf16[2,256,1,128]{1,3,2,0:T(8,128)(2,1)S(1)}, bf16[2,256,1,128]{1,3,2,0:T(8,128)(2,1)S(1)}, u32[]{:S(2)}, u32[]{:S(2)}) collective-permute-start(bf16[2,256,1,128]{1,3,2,0:T(8,128)(2,1)S(1)} %pad_maximum_fusion.1), channel_id=1, source_target_pairs={{0,2},{2,4},{4,6},{6,8},{8,10},{10,12},{12,14},{14,16},{16,18},{18... | collective-permute-start | bytes 393224 | tf_op jit(solution)/shard_map/ppermute | solution.py:15
  44.2 0.7 copy-start.7
  44.2 0.7 copy-start.16
  44.3 0.9 copy-start.13
  45.0 1.1 %copy-start.14 = (pred[256,1280]{0,1:T(8,128)(4,1)S(1)}, pred[256,1280]{0,1:T(8,128)(4,1)}, u32[]{:S(2)}) copy-start(pred[256,1280]{0,1:T(8,128)(4,1)} %fusion.13) | copy-start | bytes 983044
  48.1 2.3 %copy-start.10 = (f32[1280,1,128]{0,2,1:T(8,128)}, f32[1280,1,128]{0,2,1:T(8,128)S(1)}, u32[]{:S(2)}) copy-start(f32[1280,1,128]{0,2,1:T(8,128)S(1)} %convolution_bitcast_fusion.1) | copy-start | bytes 1966084
  49.3 1.2 %copy-start.11 = (f32[1280,1,128]{0,2,1:T(8,128)}, f32[1280,1,128]{0,2,1:T(8,128)S(1)}, u32[]{:S(2)}) copy-start(f32[1280,1,128]{0,2,1:T(8,128)S(1)} %convolution_bitcast_fusion.2) | copy-start | bytes 1966084
  51.4 10.7 %collective-permute-start.4 = (bf16[2,256,1,128]{1,3,2,0:T(8,128)(2,1)}, bf16[2,256,1,128]{1,3,2,0:T(8,128)(2,1)}, u32[]{:S(2)}, u32[]{:S(2)}) collective-permute-start(bf16[2,256,1,128]{1,3,2,0:T(8,128)(2,1)} %get-tuple-element.4), channel_id=1, source_target_pairs={{2,0},{4,2},{6,4},{8,6},{10,8},{12,10},{14,12},{16,14},{18,16},{20... | collective-permute-start | bytes 393224 | tf_op jit(solution)/shard_map/ppermute | solution.py:15
  52.7 11.5 %collective-permute-start.5 = (bf16[2,256,1,128]{1,3,2,0:T(8,128)(2,1)}, bf16[2,256,1,128]{1,3,2,0:T(8,128)(2,1)}, u32[]{:S(2)}, u32[]{:S(2)}) collective-permute-start(bf16[2,256,1,128]{1,3,2,0:T(8,128)(2,1)} %get-tuple-element.7), channel_id=1, source_target_pairs={{4,0},{6,2},{8,4},{10,6},{12,8},{14,10},{16,12},{18,14},{20,16},{2... | collective-permute-start | bytes 393224 | tf_op jit(solution)/shard_map/ppermute | solution.py:15
  54.0 12.1 %collective-permute-start.6 = (bf16[2,256,1,128]{1,3,2,0:T(8,128)(2,1)}, bf16[2,256,1,128]{1,3,2,0:T(8,128)(2,1)}, u32[]{:S(2)}, u32[]{:S(2)}) collective-permute-start(bf16[2,256,1,128]{1,3,2,0:T(8,128)(2,1)} %get-tuple-element.6), channel_id=1, source_target_pairs={{6,0},{8,2},{10,4},{12,6},{14,8},{16,10},{18,12},{20,14},{22,16},{... | collective-permute-start | bytes 393224 | tf_op jit(solution)/shard_map/ppermute | solution.py:15
  55.3 14.7 %collective-permute-start.7 = (bf16[2,256,1,128]{1,3,2,0:T(8,128)(2,1)}, bf16[2,256,1,128]{1,3,2,0:T(8,128)(2,1)}, u32[]{:S(2)}, u32[]{:S(2)}) collective-permute-start(bf16[2,256,1,128]{1,3,2,0:T(8,128)(2,1)} %get-tuple-element.5), channel_id=1, source_target_pairs={{8,0},{10,2},{12,4},{14,6},{16,8},{18,10},{20,12},{22,14},{24,16},... | collective-permute-start | bytes 393224 | tf_op jit(solution)/shard_map/ppermute | solution.py:15
  58.3 31.2 %reduce-scatter.5.cloned.1.call-start = ((), (), s32[]{:S(2)}) async-start(), calls=%async_computation.3 | async-start | bytes 2064384 | tf_op jit(solution)/shard_map/reduce_scatter | solution.py:178
  62.1 10.3 %copy-start.9 = (f32[256,128]{0,1:T(8,128)S(1)}, f32[256,128]{0,1:T(8,128)}, u32[]{:S(2)}) copy-start(f32[256,128]{0,1:T(8,128)} %copy-done.8) | copy-start | bytes 393220
  62.1 10.4 %copy-start.4 = (bf16[2688,128]{1,0:T(8,128)(2,1)S(1)}, bf16[2688,128]{1,0:T(8,128)(2,1)}, u32[]{:S(2)}) copy-start(bf16[2688,128]{1,0:T(8,128)(2,1)} %param.11) | copy-start | bytes 2064388
  75.7 1.4 %copy-start.5 = (bf16[128,2688]{1,0:T(8,128)(2,1)S(1)}, bf16[128,2688]{1,0:T(8,128)(2,1)}, u32[]{:S(2)}) copy-start(bf16[128,2688]{1,0:T(8,128)(2,1)} %param.8) | copy-start | bytes 2064388
  75.7 13.7 %copy-start.6 = (bf16[128,2688]{1,0:T(8,128)(2,1)S(1)}, bf16[128,2688]{1,0:T(8,128)(2,1)}, u32[]{:S(2)}) copy-start(bf16[128,2688]{1,0:T(8,128)(2,1)} %param.9) | copy-start | bytes 2064388
Sparse Core Ops, SparseCore 0:
  10.0 14.2 all-gather.2
  58.4 18.6 reduce-scatter.2
  79.4 10.0 reduce-scatter.4
